TPU v7x, 256 devices: a whole 4x4x8 slice. The times are simulated.
256 devices in a mesh: row: 8 (over z), col: 16 (over y, x), smp: 2 (over core).
Axes of the slice: x: 4, y: 4, z: 8, core: 2. Of those that a mesh axis runs over, the one named last changes fastest.
Arguments:
- state: float32 [8, 2048, 512], P('smp', ('row', 'col')), may hold values from -6 to 6
- noise: float32 [2, 8, 2048, 512], P(None, 'smp', ('row', 'col')), may hold values from -6 to 6
- pair: bfloat16 [2048, 2048, 128], P('row', 'col'), may hold values from -10 to 10
- contacts: int32 [16, 6], replicated, may hold values from -1 to 15, as said below
- norm_gain: float32 [512], replicated, may hold values from 0.1 to 1.9
- w_qkv: bfloat16 [512, 1536], replicated, may hold values from -0.25 to 0.25
- w_out: bfloat16 [512, 512], replicated, may hold values from -0.25 to 0.25
- w_bias: bfloat16 [128, 32], replicated, may hold values from -1.5 to 1.5
Outputs:
- denoised: float32 [8, 2048, 512], P('smp', ('row', 'col'))
Inputs may be any that keep to these rules, and one draw needn't show every extreme that they name: `contacts`: row q lists distinct blocks, q itself first, then nearby blocks more often than far ones; its first counts are blocks and the remaining slots hold -1; some row uses all 6 slots.
All inputs are finite; a program needn't handle non-finite values.
Results may differ from a plain program's by a relative error of at most 0.012.
Values may be sent and summed in bfloat16 or wider, within the bound.
A program may use at most 128 MiB of HBM per device.

v0:
```python
import jax
import jax.numpy as jnp
from jax import lax
from jax.sharding import PartitionSpec as P

STEPS = 2


def from_root(block, axis, owner):
    block = jnp.where(lax.axis_index(axis) == owner, block, jnp.zeros_like(block))
    return lax.psum(block, axis)


def body(state, noise, pair, contacts, norm_gain, w_qkv, w_out, w_bias):
    samples_dev, rows_dev, width = state.shape
    heads = w_bias.shape[1]
    head_dim = width // heads
    row_span, blk = (pair.shape[0], pair.shape[1])
    per_row = row_span // blk
    half = row_span // lax.axis_size("smp")
    own_rows = lax.dynamic_slice_in_dim(pair, lax.axis_index("smp") * half, half, 0)
    part_bias = jnp.einsum(
        "ijc,ch->hij", own_rows, w_bias, preferred_element_type=jnp.float32
    ).astype(jnp.bfloat16)
    bias = lax.all_gather(part_bias, "smp", axis=1, tiled=True).astype(jnp.float32)
    col_index = lax.axis_index("col")
    row_index = lax.axis_index("row")
    listed = lax.dynamic_slice_in_dim(contacts, row_index * per_row, per_row, 0)
    matched = jnp.any(listed == col_index, axis=1)
    allowed = jnp.repeat(matched, blk, total_repeat_length=row_span)
    busy = jnp.any(matched)
    x = state
    for step in range(STEPS):
        mean = jnp.mean(x, axis=-1, keepdims=True)
        var = jnp.mean((x - mean) ** 2, axis=-1, keepdims=True)
        normed = ((x - mean) * lax.rsqrt(var + 1e-05) * norm_gain).astype(jnp.bfloat16)
        qkv = jnp.dot(normed, w_qkv, preferred_element_type=jnp.float32).astype(jnp.bfloat16)
        block_rows = lax.all_gather(qkv, "col", axis=1, tiled=True)
        offset = col_index % per_row * blk
        mine = lax.dynamic_slice_in_dim(block_rows[..., width:], offset, blk, 1)
        keyval = from_root(mine, "row", col_index // per_row)
        queries = block_rows[..., :width].reshape(samples_dev, row_span, heads, head_dim)
        keys = keyval[..., :width].reshape(samples_dev, blk, heads, head_dim)
        values = keyval[..., width:].reshape(samples_dev, blk, heads, head_dim)

        def attend(unused):
            scores = (
                jnp.einsum("srhd,skhd->hsrk", queries, keys, preferred_element_type=jnp.float32)
                * 0.25
                + bias[:, None]
            )
            m_raw = jnp.max(scores, axis=-1)
            m_blk = jnp.where(allowed[None, None, :], m_raw, jnp.float32(-1e30))
            probs = jnp.where(
                allowed[None, None, :, None], jnp.exp(scores - m_raw[..., None]), jnp.float32(0.0)
            )
            totals = jnp.sum(probs, axis=-1)
            outputs = jnp.einsum(
                "hsrk,skhd->srhd",
                probs.astype(jnp.bfloat16),
                values,
                preferred_element_type=jnp.float32,
            )
            return (
                m_blk.transpose(1, 2, 0),
                totals.transpose(1, 2, 0),
                outputs.reshape(samples_dev, row_span, width),
            )

        def skipped(unused):
            return (
                jnp.full((samples_dev, row_span, heads), -1e30, jnp.float32),
                jnp.zeros((samples_dev, row_span, heads), jnp.float32),
                jnp.zeros((samples_dev, row_span, width), jnp.float32),
            )

        m_blk, totals, outputs = lax.cond(busy, attend, skipped, 0)
        top = lax.pmax(m_blk.astype(jnp.bfloat16), "col").astype(m_blk.dtype)
        weight = jnp.exp(m_blk - top)
        scaled = (
            outputs.reshape(samples_dev, row_span, heads, head_dim) * weight[..., None]
        ).reshape(samples_dev, row_span, width)
        summed, acc = (
            lax.psum_scatter(totals * weight, "col", scatter_dimension=1, tiled=True),
            lax.psum_scatter(scaled, "col", scatter_dimension=1, tiled=True),
        )
        attn = (acc.reshape(samples_dev, rows_dev, heads, head_dim) / summed[..., None]).reshape(
            samples_dev, rows_dev, width
        )
        attn = attn.astype(jnp.bfloat16)
        out = jnp.dot(attn, w_out, preferred_element_type=jnp.float32)
        x = x + out + 0.5 * 0.5**step * noise[step]
    return x


def solution(mesh):
    in_specs = (
        P("smp", ("row", "col"), None),
        P(None, "smp", ("row", "col"), None),
        P("row", "col", None),
        P(),
        P(),
        P(),
        P(),
        P(),
    )
    out_specs = P("smp", ("row", "col"), None)
    return jax.shard_map(body, mesh=mesh, in_specs=in_specs, out_specs=out_specs, check_vma=False)
```

profile of v0, /device:TPU:1, one launch (start us, length us, event | category | flops | bytes accessed | tf_op | source)
XLA Modules:
  0.0 770.3 jit_solution(14538606355737976069)
XLA Ops:
  8.7 2.0 convolution_convert_fusion.1
  10.8 4.8 fusion.23
  15.7 51.2 %all-gather.4.cloned.1.call-done = bf16[4,256,1536]{2,1,0:T(8,128)(2,1)} async-done(((bf16[4,16,1536]{2,1,0:T(8,128)(2,1)}), bf16[4,256,1536]{2,1,0:T(8,128)(2,1)}) %all-gather.4.cloned.1.call-update) | async-done | bytes 3145744 | tf_op jit(solution)/shard_map/all_gather | solution.py:38
  66.9 1.6 slice-done
  73.0 11.8 %all-gather.6.cloned.1.call-done = bf16[32,256,128]{2,0,1:T(8,128)(2,1)} async-done(((bf16[32,128,128]{2,0,1:T(8,128)(2,1)}), bf16[32,256,128]{2,0,1:T(8,128)(2,1)}) %all-gather.6.cloned.1.call-update) | async-done | bytes 2097168 | tf_op jit(solution)/shard_map/all_gather | solution.py:25
  84.8 4.1 convert_element_type.54
  88.9 70.4 %all-reduce.13.cloned.1.call-done = bf16[4,128,1024]{2,1,0:T(8,128)(2,1)} async-done(((bf16[4,128,1024]{2,1,0:T(8,128)(2,1)}), bf16[4,128,1024]{2,1,0:T(8,128)(2,1)}) %all-reduce.13.cloned.1.call-update) | async-done | bytes 1048592 | tf_op jit(solution)/shard_map/psum | solution.py:11
  159.4 29.7 %conditional.2 = (f32[4,256,512]{1,2,0:T(8,128)}, f32[4,256,32]{1,2,0:T(8,128)}, f32[4,256,32]{1,2,0:T(8,128)}) conditional(s32[]{:T(128)} %convert_element_type.49, () %tuple.25, (pred[256]{0:T(512)(128)(4,1)S(1)}, bf16[4,256,1536]{2,1,0:T(8,128)(2,1)}, bf16[4,128,1024]{2,1,0:T(8,128)(2,1)}, f32[32,256,128]{2,0,1:T(8,128)}) %tuple.26), branch_computations={%region_5.6_spmd, %region_6.9_spmd} | conditional | flops 306151424 | bytes 102367824 | solution.py:77
  159.4 5.3 copy.95
  164.6 1.6 copy.94
  167.1 4.6 copy.93
  173.1 5.4 fusion
  178.5 6.6 fusion.2
  186.5 2.6 fusion.3
  190.7 93.2 %all-reduce.15.cloned.1.call-done = bf16[4,256,32]{1,2,0:T(8,128)(2,1)} async-done(((bf16[4,256,32]{1,2,0:T(8,128)(2,1)}), bf16[4,256,32]{1,2,0:T(8,128)(2,1)}) %all-reduce.15.cloned.1.call-update) | async-done | bytes 65552 | tf_op jit(solution)/shard_map/pmax | solution.py:78
  284.9 3.2 bitcast_multiply_fusion.1
  288.1 3.1 copy.98
  293.6 102.3 %all-reduce.23.cloned.1.call-done = (f32[4,256,32]{2,0,1:T(4,128)}, f32[4,256,512]{2,0,1:T(4,128)}) async-done(((f32[4,256,32]{2,0,1:T(4,128)}, f32[4,256,512]{2,0,1:T(4,128)}), (f32[4,256,32]{2,0,1:T(4,128)}, f32[4,256,512]{2,0,1:T(4,128)})) %all-reduce.23.cloned.1.call-update) | async-done | bytes 2228240
  401.9 52.4 %all-gather.8.cloned.1.call-done = bf16[4,256,1536]{2,1,0:T(8,128)(2,1)} async-done(((bf16[4,16,1536]{2,1,0:T(8,128)(2,1)}), bf16[4,256,1536]{2,1,0:T(8,128)(2,1)}) %all-gather.8.cloned.1.call-update) | async-done | bytes 3145744 | tf_op jit(solution)/shard_map/all_gather | solution.py:38
  454.4 1.6 slice-done.1
  457.3 71.1 %all-reduce.17.cloned.1.call-done = bf16[4,128,1024]{2,1,0:T(8,128)(2,1)} async-done(((bf16[4,128,1024]{2,1,0:T(8,128)(2,1)}), bf16[4,128,1024]{2,1,0:T(8,128)(2,1)}) %all-reduce.17.cloned.1.call-update) | async-done | bytes 1048592 | tf_op jit(solution)/shard_map/psum | solution.py:11
  528.4 25.1 %conditional.3 = (f32[4,256,512]{1,2,0:T(8,128)}, f32[4,256,32]{1,2,0:T(8,128)S(1)}, f32[4,256,32]{1,2,0:T(8,128)S(1)}) conditional(s32[]{:T(128)} %convert_element_type.49, () %tuple.27, (pred[256]{0:T(512)(128)(4,1)S(1)}, bf16[4,256,1536]{2,1,0:T(8,128)(2,1)}, bf16[4,128,1024]{2,1,0:T(8,128)(2,1)}, f32[32,256,128]{2,0,1:T(8,128)}) %tuple.28), branch_computations={%region_15.16_spmd, %region_16.19_spmd} | conditional | flops 306151424 | bytes 106037840 | solution.py:77
  528.4 5.4 copy.105
  534.5 4.6 copy.103
  540.5 4.5 fusion.8
  545.0 5.8 fusion.10
  550.9 2.6 fusion.11
  554.2 93.3 %all-reduce.19.cloned.1.call-done = bf16[4,256,32]{1,2,0:T(8,128)(2,1)} async-done(((bf16[4,256,32]{1,2,0:T(8,128)(2,1)}), bf16[4,256,32]{1,2,0:T(8,128)(2,1)}) %all-reduce.19.cloned.1.call-update) | async-done | bytes 65552 | tf_op jit(solution)/shard_map/pmax | solution.py:78
  648.4 3.1 bitcast_multiply_fusion
  651.5 3.2 copy.108
  655.7 103.6 %all-reduce.21.cloned.1.call-done = (f32[4,256,32]{2,0,1:T(4,128)}, f32[4,256,512]{2,0,1:T(4,128)}) async-done(((f32[4,256,32]{2,0,1:T(4,128)}, f32[4,256,512]{2,0,1:T(4,128)}), (f32[4,256,32]{2,0,1:T(4,128)}, f32[4,256,512]{2,0,1:T(4,128)})) %all-reduce.21.cloned.1.call-update) | async-done | bytes 2228240
  762.0 1.8 fusion.26
  (87 shorter events, 28.6 us)
Async XLA Ops:
  6.5 2.2 copy-start
  6.5 60.4 %all-gather.4.cloned.1.call-start = ((), (), s32[]{:S(2)}) async-start(), calls=%async_computation | async-start | bytes 3342336 | tf_op jit(solution)/shard_map/all_gather | solution.py:38
  10.8 74.0 %all-gather.6.cloned.1.call-start = ((), (), s32[]{:S(2)}) async-start(), calls=%async_computation.2 | async-start | bytes 3145728 | tf_op jit(solution)/shard_map/all_gather | solution.py:25
  15.6 54.2 %copy-start.9 = (s32[16,6]{0,1:T(8,128)S(1)}, s32[16,6]{0,1:T(8,128)}, u32[]{:S(2)}) copy-start(s32[16,6]{0,1:T(8,128)} %param.17) | copy-start | bytes 1156
  15.6 143.7 %all-reduce.13.cloned.1.call-start = ((), (), s32[]{:S(2)}) async-start(), calls=%async_computation.1 | async-start | bytes 2097152 | tf_op jit(solution)/shard_map/psum | solution.py:11
  66.9 1.6 slice-start
  69.7 214.2 %all-reduce.15.cloned.1.call-start = ((), (), s32[]{:S(2)}) async-start(), calls=%async_computation.3 | async-start | bytes 131072 | tf_op jit(solution)/shard_map/pmax | solution.py:78
  173.1 5.4 copy-start.2
  178.5 6.6 copy-start.6
  190.6 205.4 %all-reduce.23.cloned.1.call-start = ((), (), s32[]{:S(2)}) async-start(), calls=%async_computation.8 | async-start | bytes 5242880
  288.1 4.3 copy-start.10
  288.1 111.2 %copy-start.4 = (f32[4,16,512]{2,1,0:T(8,128)S(1)}, f32[4,16,512]{2,1,0:T(8,128)}, u32[]{:S(2)}) copy-start(f32[4,16,512]{2,1,0:T(8,128)} %param.14) | copy-start | bytes 393220
  288.1 111.2 %copy-start.5 = (bf16[512,512]{1,0:T(8,128)(2,1)S(1)}, bf16[512,512]{1,0:T(8,128)(2,1)}, u32[]{:S(2)}) copy-start(bf16[512,512]{1,0:T(8,128)(2,1)} %param.20) | copy-start | bytes 1572868
  291.2 109.5 %copy-start.8 = (f32[512]{0:T(512)S(1)}, f32[512]{0:T(512)}, u32[]{:S(2)}) copy-start(f32[512]{0:T(512)} %param.18) | copy-start | bytes 6148
  292.3 162.0 %all-gather.8.cloned.1.call-start = ((), (), s32[]{:S(2)}) async-start(), calls=%async_computation.4 | async-start | bytes 3342336 | tf_op jit(solution)/shard_map/all_gather | solution.py:38
  401.9 126.5 %all-reduce.17.cloned.1.call-start = ((), (), s32[]{:S(2)}) async-start(), calls=%async_computation.5 | async-start | bytes 2097152 | tf_op jit(solution)/shard_map/psum | solution.py:11
  454.4 1.6 slice-start.1
  457.2 190.3 %all-reduce.19.cloned.1.call-start = ((), (), s32[]{:S(2)}) async-start(), calls=%async_computation.6 | async-start | bytes 131072 | tf_op jit(solution)/shard_map/pmax | solution.py:78
  528.4 5.4 copy-start.7
  540.4 4.5 copy-start.3
  554.2 205.2 %all-reduce.21.cloned.1.call-start = ((), (), s32[]{:S(2)}) async-start(), calls=%async_computation.7 | async-start | bytes 5242880
  651.5 112.3 %copy-start.1 = (bf16[512,1536]{1,0:T(8,128)(2,1)S(1)}, bf16[512,1536]{1,0:T(8,128)(2,1)}, u32[]{:S(2)}) copy-start(bf16[512,1536]{1,0:T(8,128)(2,1)} %param.19) | copy-start | bytes 4718596
Sparse Core Ops, SparseCore 0:
  10.9 55.9 all-gather.3
  68.7 16.0 all-gather.5
  87.2 72.1 all-reduce.12
  190.7 93.1 all-reduce.14
  292.5 103.4 all-reduce.22
  402.0 52.3 all-gather.7
  457.3 71.0 all-reduce.16
  554.3 93.1 all-reduce.18
  655.8 103.4 all-reduce.20
where the time goes:
time: 771 us; the launch traced here: 770 us
  waiting for transfers between devices  650 us (84%)
  local copies, waits for them, and re-layouts  45.9 us (6%)
  other arithmetic  33.8 us (4%)
  matrix products  26 us (3%)
  between operations  14.7 us (2%)
    unnamed x11, waiting for transfers between devices  206 us
    pmax x2, waiting for transfers between devices, body(): top = lax.pmax(m_blk.astype(jnp.bfloat16), 'col').astype(m_blk.dtype)  187 us
    psum x2, waiting for transfers between devices, from_root(): return lax.psum(block, axis)  142 us
    all_gather x2, waiting for transfers between devices, body(): block_rows = lax.all_gather(qkv, 'col', axis=1, tiled=True)  104 us
    another operation x6, local copies, waits for them, and re-layouts  22.2 us
  transfers between devices with their start and end apart: 9, of which 9 were waited for; matrix products, arithmetic and copies ran while one was open for 2% of the time, Pallas kernels for 0%

commit v1 on v0

--- a/solution.py
+++ b/solution.py
@@ -8,7 +8,7 @@
 
 def from_root(block, axis, owner):
     block = jnp.where(lax.axis_index(axis) == owner, block, jnp.zeros_like(block))
-    return lax.psum(block, axis)
+    return jnp.sum(lax.all_gather(block, axis), axis=0)
 
 
 def body(state, noise, pair, contacts, norm_gain, w_qkv, w_out, w_bias):

time: 771 us -> 820 us (1.064)
  waiting for transfers between devices: 650 us -> 685 us
  other arithmetic: 33.8 us -> 45.2 us
    all_gather x0 -> x2, waiting for transfers between devices: none -> 186 us  [from_root(): return jnp.sum(lax.all_gather(block, axis), axis=0)]
    psum x2 -> x0, waiting for transfers between devices: 142 us -> none  [from_root(): return lax.psum(block, axis)]
    reduce_sum x0 -> x2, other arithmetic: none -> 11.2 us  [from_root(): return jnp.sum(lax.all_gather(block, axis), axis=0)]
where the time goes in v1:
time: 820 us; the launch traced here: 819 us
  waiting for transfers between devices  685 us (84%)
  local copies, waits for them, and re-layouts  47.4 us (6%)
  other arithmetic  45.2 us (6%)
  matrix products  26 us (3%)
  between operations  14.7 us (2%)
    unnamed x11, waiting for transfers between devices  206 us
    all_gather x2, waiting for transfers between devices, from_root(): return jnp.sum(lax.all_gather(block, axis), axis=0)  186 us
    pmax x2, waiting for transfers between devices, body(): top = lax.pmax(m_blk.astype(jnp.bfloat16), 'col').astype(m_blk.dtype)  178 us
    all_gather x2, waiting for transfers between devices, body(): block_rows = lax.all_gather(qkv, 'col', axis=1, tiled=True)  104 us
    another operation x6, local copies, waits for them, and re-layouts  21.8 us
  transfers between devices with their start and end apart: 9, of which 9 were waited for; matrix products, arithmetic and copies ran while one was open for 2% of the time, Pallas kernels for 0%

profile of v1, /device:TPU:1, one launch (start us, length us, event | category | flops | bytes accessed | tf_op | source)
XLA Modules:
  0.0 819.2 jit_solution(8088591402080817758)
XLA Ops:
  8.7 2.0 convolution_convert_fusion.1
  10.8 4.8 fusion.23
  15.7 51.2 %all-gather.8.cloned.1.call-done = bf16[4,256,1536]{2,1,0:T(8,128)(2,1)} async-done(((bf16[4,16,1536]{2,1,0:T(8,128)(2,1)}), bf16[4,256,1536]{2,1,0:T(8,128)(2,1)}) %all-gather.8.cloned.1.call-update) | async-done | bytes 3145744 | tf_op jit(solution)/shard_map/all_gather | solution.py:38
  73.1 11.7 %all-gather.10.cloned.1.call-done = bf16[32,256,128]{2,0,1:T(8,128)(2,1)} async-done(((bf16[32,128,128]{2,0,1:T(8,128)(2,1)}), bf16[32,256,128]{2,0,1:T(8,128)(2,1)}) %all-gather.10.cloned.1.call-update) | async-done | bytes 2097168 | tf_op jit(solution)/shard_map/all_gather | solution.py:25
  84.8 4.1 convert_element_type.58
  88.9 92.2 %all-gather.14.cloned.1.call-done = bf16[32,128,1024]{2,1,0:T(8,128)(2,1)} async-done(((bf16[4,128,1024]{2,1,0:T(8,128)(2,1)}), bf16[32,128,1024]{2,1,0:T(8,128)(2,1)}) %all-gather.14.cloned.1.call-update) | async-done | bytes 8388624 | tf_op jit(solution)/shard_map/all_gather | solution.py:11
  181.1 5.6 reduce_sum.80
  186.7 30.6 %conditional.2 = (f32[4,256,512]{1,2,0:T(8,128)}, f32[4,256,32]{1,2,0:T(8,128)}, f32[4,256,32]{1,2,0:T(8,128)}) conditional(s32[]{:T(128)} %convert_element_type.53, () %tuple.25, (pred[256]{0:T(512)(128)(4,1)S(1)}, bf16[4,256,1536]{2,1,0:T(8,128)(2,1)}, bf16[4,128,1024]{2,1,0:T(8,128)(2,1)S(1)}, f32[32,256,128]{2,0,1:T(8,128)}) %tuple.26), branch_computations={%region_5.6_spmd, %region_6.9_spmd} | conditional | flops 306151424 | bytes 102367824 | solution.py:77
  186.8 5.3 copy.91
  193.3 2.1 fusion.47
  195.4 4.6 copy.89
  201.3 5.4 fusion
  206.8 6.6 fusion.2
  214.8 2.6 fusion.3
  218.9 89.2 %all-reduce.11.cloned.1.call-done = bf16[4,256,32]{1,2,0:T(8,128)(2,1)} async-done(((bf16[4,256,32]{1,2,0:T(8,128)(2,1)}), bf16[4,256,32]{1,2,0:T(8,128)(2,1)}) %all-reduce.11.cloned.1.call-update) | async-done | bytes 65552 | tf_op jit(solution)/shard_map/pmax | solution.py:78
  309.1 3.2 bitcast_multiply_fusion.1
  312.3 3.1 copy.94
  317.9 102.2 %all-reduce.17.cloned.1.call-done = (f32[4,256,32]{2,0,1:T(4,128)}, f32[4,256,512]{2,0,1:T(4,128)}) async-done(((f32[4,256,32]{2,0,1:T(4,128)}, f32[4,256,512]{2,0,1:T(4,128)}), (f32[4,256,32]{2,0,1:T(4,128)}, f32[4,256,512]{2,0,1:T(4,128)})) %all-reduce.17.cloned.1.call-update) | async-done | bytes 2228240
  426.1 52.4 %all-gather.12.cloned.1.call-done = bf16[4,256,1536]{2,1,0:T(8,128)(2,1)} async-done(((bf16[4,16,1536]{2,1,0:T(8,128)(2,1)}), bf16[4,256,1536]{2,1,0:T(8,128)(2,1)}) %all-gather.12.cloned.1.call-update) | async-done | bytes 3145744 | tf_op jit(solution)/shard_map/all_gather | solution.py:38
  481.4 93.5 %all-gather.16.cloned.1.call-done = bf16[32,128,1024]{2,1,0:T(8,128)(2,1)} async-done(((bf16[4,128,1024]{2,1,0:T(8,128)(2,1)}), bf16[32,128,1024]{2,1,0:T(8,128)(2,1)}) %all-gather.16.cloned.1.call-update) | async-done | bytes 8388624 | tf_op jit(solution)/shard_map/all_gather | solution.py:11
  574.8 5.6 reduce_sum.83
  580.5 25.9 %conditional.3 = (f32[4,256,512]{1,2,0:T(8,128)}, f32[4,256,32]{1,2,0:T(8,128)S(1)}, f32[4,256,32]{1,2,0:T(8,128)S(1)}) conditional(s32[]{:T(128)} %convert_element_type.53, () %tuple.27, (pred[256]{0:T(512)(128)(4,1)S(1)}, bf16[4,256,1536]{2,1,0:T(8,128)(2,1)}, bf16[4,128,1024]{2,1,0:T(8,128)(2,1)S(1)}, f32[32,256,128]{2,0,1:T(8,128)}) %tuple.28), branch_computations={%region_15.16_spmd, %region_16.19_spmd} | conditional | flops 306151424 | bytes 103940688 | solution.py:77
  580.5 5.3 copy.101
  587.3 4.7 copy.99
  593.3 4.5 fusion.8
  597.9 5.8 fusion.10
  603.8 2.6 fusion.11
  607.1 89.2 %all-reduce.13.cloned.1.call-done = bf16[4,256,32]{1,2,0:T(8,128)(2,1)} async-done(((bf16[4,256,32]{1,2,0:T(8,128)(2,1)}), bf16[4,256,32]{1,2,0:T(8,128)(2,1)}) %all-reduce.13.cloned.1.call-update) | async-done | bytes 65552 | tf_op jit(solution)/shard_map/pmax | solution.py:78
  697.3 3.1 bitcast_multiply_fusion
  700.4 3.2 copy.104
  704.6 103.6 %all-reduce.15.cloned.1.call-done = (f32[4,256,32]{2,0,1:T(4,128)}, f32[4,256,512]{2,0,1:T(4,128)}) async-done(((f32[4,256,32]{2,0,1:T(4,128)}, f32[4,256,512]{2,0,1:T(4,128)}), (f32[4,256,32]{2,0,1:T(4,128)}, f32[4,256,512]{2,0,1:T(4,128)})) %all-reduce.15.cloned.1.call-update) | async-done | bytes 2228240
  810.9 1.8 fusion.26
  (91 shorter events, 33.3 us)
Async XLA Ops:
  6.5 2.2 copy-start
  6.5 60.4 %all-gather.8.cloned.1.call-start = ((), (), s32[]{:S(2)}) async-start(), calls=%async_computation | async-start | bytes 3342336 | tf_op jit(solution)/shard_map/all_gather | solution.py:38
  10.8 74.0 %all-gather.10.cloned.1.call-start = ((), (), s32[]{:S(2)}) async-start(), calls=%async_computation.1 | async-start | bytes 3145728 | tf_op jit(solution)/shard_map/all_gather | solution.py:25
  15.6 54.2 %copy-start.10 = (s32[16,6]{0,1:T(8,128)S(1)}, s32[16,6]{0,1:T(8,128)}, u32[]{:S(2)}) copy-start(s32[16,6]{0,1:T(8,128)} %param.17) | copy-start | bytes 1156
  15.7 165.4 %all-gather.14.cloned.1.call-start = ((), (), s32[]{:S(2)}) async-start(), calls=%async_computation.5 | async-start | bytes 9437184 | tf_op jit(solution)/shard_map/all_gather | solution.py:11
  66.9 1.6 slice-start
  69.7 238.4 %all-reduce.11.cloned.1.call-start = ((), (), s32[]{:S(2)}) async-start(), calls=%async_computation.2 | async-start | bytes 131072 | tf_op jit(solution)/shard_map/pmax | solution.py:78
  201.3 5.4 copy-start.2
  206.8 6.6 copy-start.7
  218.9 201.3 %all-reduce.17.cloned.1.call-start = ((), (), s32[]{:S(2)}) async-start(), calls=%async_computation.8 | async-start | bytes 5242880
  312.3 4.4 copy-start.11
  312.3 111.1 %copy-start.4 = (f32[4,16,512]{2,1,0:T(8,128)S(1)}, f32[4,16,512]{2,1,0:T(8,128)}, u32[]{:S(2)}) copy-start(f32[4,16,512]{2,1,0:T(8,128)} %param.14) | copy-start | bytes 393220
  312.3 111.1 %copy-start.5 = (bf16[512,512]{1,0:T(8,128)(2,1)S(1)}, bf16[512,512]{1,0:T(8,128)(2,1)}, u32[]{:S(2)}) copy-start(bf16[512,512]{1,0:T(8,128)(2,1)} %param.20) | copy-start | bytes 1572868
  315.4 109.5 %copy-start.9 = (f32[512]{0:T(512)S(1)}, f32[512]{0:T(512)}, u32[]{:S(2)}) copy-start(f32[512]{0:T(512)} %param.18) | copy-start | bytes 6148
  316.5 162.1 %all-gather.12.cloned.1.call-start = ((), (), s32[]{:S(2)}) async-start(), calls=%async_computation.3 | async-start | bytes 3342336 | tf_op jit(solution)/shard_map/all_gather | solution.py:38
  426.0 148.8 %all-gather.16.cloned.1.call-start = ((), (), s32[]{:S(2)}) async-start(), calls=%async_computation.6 | async-start | bytes 9437184 | tf_op jit(solution)/shard_map/all_gather | solution.py:11
  478.5 1.6 slice-start.1
  481.3 215.0 %all-reduce.13.cloned.1.call-start = ((), (), s32[]{:S(2)}) async-start(), calls=%async_computation.4 | async-start | bytes 131072 | tf_op jit(solution)/shard_map/pmax | solution.py:78
  587.3 6.0 copy-start.6
  593.3 4.6 copy-start.3
  606.4 90.0 %copy-start.8 = (f32[4,256,32]{1,2,0:T(8,128)}, f32[4,256,32]{1,2,0:T(8,128)S(1)}, u32[]{:S(2)}) copy-start(f32[4,256,32]{1,2,0:T(8,128)S(1)} %get-tuple-element.110) | copy-start | bytes 393220
  607.1 201.2 %all-reduce.15.cloned.1.call-start = ((), (), s32[]{:S(2)}) async-start(), calls=%async_computation.7 | async-start | bytes 5242880
  700.4 112.3 %copy-start.1 = (bf16[512,1536]{1,0:T(8,128)(2,1)S(1)}, bf16[512,1536]{1,0:T(8,128)(2,1)}, u32[]{:S(2)}) copy-start(bf16[512,1536]{1,0:T(8,128)(2,1)} %param.19) | copy-start | bytes 4718596
Sparse Core Ops, SparseCore 0:
  10.9 55.9 all-gather.7
  68.7 16.0 all-gather.9
  86.6 94.4 all-gather.13
  219.0 89.0 all-reduce.10
  316.6 103.5 all-reduce.16
  426.2 52.3 all-gather.11
  481.5 93.3 all-gather.15
  607.2 89.1 all-reduce.12
  704.8 103.4 all-reduce.14
